TPU v7x, 32 devices: a whole 2x2x4 slice. The times are simulated.
32 devices in a mesh: kx: 2 (over x), ky: 8 (over z, y), af: 2 (over core).
Axes of the slice: x: 2, y: 2, z: 4, core: 2. Of those that a mesh axis runs over, the one named last changes fastest.
Arguments:
- vertex: float32 [2, 2, 8, 768, 768], P(None, 'kx', 'ky', 'af'), may hold values from -1.2 to 1.2
- bare_vertex: float32 [2, 2, 8, 768, 768], P(None, 'kx', 'ky', 'af'), may hold values from -1.2 to 1.2
- bubble_direct: float32 [2, 2, 8, 768], P(None, 'kx', 'ky'), may hold values from 0.1 to 1
- bubble_crossed: float32 [2, 2, 8, 768], P(None, 'kx', 'ky'), may hold values from 0.1 to 1
- shear_in: int32 [2, 768], replicated, may hold values from 0 to 7, as said below
- shear_out: int32 [2, 768], replicated, may hold values from 0 to 7, as said below
Outputs:
- updated: float32 [2, 2, 8, 768, 768], P(None, 'kx', 'ky', 'af')
Inputs may be any that keep to these rules, and one draw needn't show every extreme that they name: `shear_in`: row 0 holds each matrix row's shift of the first momentum component (below 4), row 1 that of the second (below 8). Within each half of the 768 rows, every pair (first shift mod 2, second shift) occurs for exactly 24 rows. `shear_out`: same structure as shear_in.
All inputs are finite; a program needn't handle non-finite values.
Results may differ from a plain program's by a relative error of at most 0.000082.
Values sent between devices are 32-bit elements; how exact they have to be, the bound alone decides.
No kernel may reach another device: no remote copies, remote signals or barrier semaphores. Data moves between devices by JAX's collectives and lax.ppermute only.
A program may use at most 64 MiB of HBM per device.

v0:
```python
import jax
import jax.numpy as jnp
from jax import lax
from jax.sharding import PartitionSpec as P

mixing = 0.5


def ladder(vertex_rows, bubble_row):
    scaled = vertex_rows * bubble_row[:, None, :]
    whole = lax.all_gather(vertex_rows, "af", axis=1, tiled=True)
    return jnp.einsum(
        "hrk,hkc->hrc",
        scaled,
        whole,
        precision=lax.Precision.HIGHEST,
        preferred_element_type=jnp.float32,
    )


def pack_rows(data, target):
    row_order = jnp.argsort(target, stable=True)
    return jnp.take(data, row_order, axis=1)


def unpack_rows(data, anchor):
    row_order = jnp.argsort(anchor, stable=True)
    inverse = jnp.argsort(row_order, stable=True)
    return jnp.take(data, inverse, axis=1)


def crossing(vertex_rows, shear_table):
    item_count = vertex_rows.shape[0]
    row_count = vertex_rows.shape[1]
    row_first = lax.axis_index("af") * row_count
    shift_x = lax.dynamic_slice_in_dim(shear_table[0], row_first, row_count)
    shift_y = lax.dynamic_slice_in_dim(shear_table[1], row_first, row_count)
    width_x = lax.axis_size("kx")
    width_y = lax.axis_size("ky")
    kx_index = lax.axis_index("kx")
    ky_index = lax.axis_index("ky")
    carry_bit = (kx_index + shift_x % width_x >= width_x).astype(jnp.int32)
    item_turn = (shift_x // width_x + carry_bit) % item_count
    turned = vertex_rows
    rolled = jnp.roll(vertex_rows, 1, axis=0)
    turned = jnp.where((item_turn == 1)[None, :, None], rolled, turned)
    target_x = (kx_index + shift_x) % width_x
    target_y = (ky_index + shift_y) % width_y
    anchor_x = (kx_index - shift_x) % width_x
    anchor_y = (ky_index - shift_y) % width_y
    arrived = lax.all_to_all(
        pack_rows(turned, target_x * width_y + target_y),
        ("kx", "ky"),
        split_axis=1,
        concat_axis=1,
        tiled=True,
    )
    return unpack_rows(arrived, anchor_x * width_y + anchor_y)


def body(vertex, bare_vertex, bubble_direct, bubble_crossed, shear_in, shear_out):
    item_count = vertex.shape[0]
    row_count = vertex.shape[3]
    columns = vertex.shape[4]
    local_field = vertex.reshape(item_count, row_count, columns)
    local_bare = bare_vertex.reshape(item_count, row_count, columns)
    direct_bubble = bubble_direct.reshape(item_count, columns)
    crossed_bubble = bubble_crossed.reshape(item_count, columns)
    direct_ladder = ladder(local_field, direct_bubble)
    crossed = crossing(local_field, shear_in)
    crossed_ladder = ladder(crossed, crossed_bubble)
    returned = crossing(crossed_ladder, shear_out)
    updated = (1.0 - mixing) * local_field + mixing * (local_bare + direct_ladder + returned)
    return updated.reshape(vertex.shape)


def solution(mesh):
    placed = (
        P(None, "kx", "ky", "af", None),
        P(None, "kx", "ky", "af", None),
        P(None, "kx", "ky", None),
        P(None, "kx", "ky", None),
        P(),
        P(),
    )
    return jax.shard_map(
        body, mesh=mesh, in_specs=placed, out_specs=P(None, "kx", "ky", "af", None), check_vma=False
    )
```

profile of v0, /device:TPU:0, one launch (start us, length us, event | category | flops | bytes accessed | tf_op | source)
XLA Modules:
  0.0 213.0 jit_solution(2897367871155619934)
XLA Ops:
  6.5 0.8 fusion.44
  7.4 3.8 %sort.87 = (s32[384]{0:T(512)}, s32[384]{0:T(512)S(1)}) sort(s32[384]{0:T(512)S(1)} %get-tuple-element.33, s32[384]{0:T(512)S(1)} %iota.19), dimensions={0}, to_apply=%region_0.1 | sort | flops 3456 | bytes 6144 | tf_op jit(solution)/shard_map/jit(argsort)/sort | solution.py:22
  11.2 1.9 slice_bitcast_fusion.1
  13.1 0.4 copy-done
  13.6 0.5 maximum_select_fusion
  14.1 3.2 %copy.10 = f32[2,384,768]{2,0,1:T(2,128)} copy(f32[2,384,768]{2,1,0:T(8,128)S(1)} %maximum_select_fusion) | data formatting | bytes 4718592 | tf_op jit(solution)/shard_map/jit(_where)/select_n | solution.py:46
  17.3 5.1 %gather_fusion = f32[384,2,768]{2,1,0:T(2,128)S(1)} fusion(f32[2,384,768]{2,0,1:T(2,128)} %copy.10, s32[1024]{0:T(1024)S(1)} %pad_clamp_fusion.3), kind=kCustom, calls=%fused_computation.clone | custom fusion | bytes 4720128 | tf_op jit(solution)/shard_map/jit(_take)/gather | solution.py:23
  22.4 2.8 %select_bitcast_fusion.1 = f32[2,384,768]{2,0,1:T(2,128)} fusion(f32[384,2,768]{2,1,0:T(2,128)S(1)} %gather_fusion, pred[384]{0:T(512)(128)(4,1)S(1)} %compare_and_fusion.3), kind=kLoop, calls=%fused_computation.18 | loop fusion | flops 589824 | bytes 4718976 | tf_op jit(solution)/shard_map/jit(_take)/select_n | solution.py:23
  25.1 8.3 %all-to-all-start = ((f32[2,384,768]{2,0,1:T(2,128)}), f32[2,384,768]{2,0,1:T(2,128)S(1)}, u32[]{:S(2)}, u32[]{:S(2)}) async-start(f32[2,384,768]{2,0,1:T(2,128)} %select_bitcast_fusion.1), calls=%async_computation | async-start | bytes 4718592 | tf_op jit(solution)/shard_map/all_to_all | solution.py:51
  33.5 0.0 all-gather.4.cloned.1.call-start
  33.5 3.8 %sort.88 = (s32[384]{0:T(512)}, s32[384]{0:T(512)S(1)}) sort(s32[384]{0:T(512)S(1)} %get-tuple-element.32, s32[384]{0:T(512)S(1)} %iota.20), dimensions={0}, to_apply=%region_1.3 | sort | flops 3456 | bytes 6144 | tf_op jit(solution)/shard_map/jit(argsort)/sort | solution.py:27
  37.3 3.8 %sort.89 = (s32[384]{0:T(512)}, s32[384]{0:T(512)S(1)}) sort(s32[384]{0:T(512)S(1)} %get-tuple-element.13, s32[384]{0:T(512)S(1)} %iota.21), dimensions={0}, to_apply=%region_2.4 | sort | flops 3456 | bytes 6144 | tf_op jit(solution)/shard_map/jit(argsort)/sort | solution.py:28
  41.1 44.8 %all-to-all-done = f32[2,384,768]{2,0,1:T(2,128)S(1)} async-done(((f32[2,384,768]{2,0,1:T(2,128)}), f32[2,384,768]{2,0,1:T(2,128)S(1)}, u32[]{:S(2)}, u32[]{:S(2)}) %all-to-all-start) | async-done | bytes 2359328 | tf_op jit(solution)/shard_map/all_to_all | solution.py:51
  85.9 5.2 %gather_fusion.1 = f32[384,2,768]{2,1,0:T(2,128)} fusion(f32[2,384,768]{2,0,1:T(2,128)S(1)} %all-to-all-done, s32[1024]{0:T(1024)S(1)} %pad_clamp_fusion.2), kind=kCustom, calls=%fused_computation.1.clone | custom fusion | bytes 4720128 | tf_op jit(solution)/shard_map/jit(_take)/gather | solution.py:29
  91.1 3.3 %fusion.5 = f32[2,384,768]{2,1,0:T(8,128)} fusion(f32[384,2,768]{2,1,0:T(2,128)} %gather_fusion.1, pred[384]{0:T(512)(128)(4,1)S(1)} %compare_and_fusion.2), kind=kLoop, calls=%fused_computation.16 | loop fusion | flops 589824 | bytes 4718976 | tf_op jit(solution)/shard_map/jit(_take)/select_n | solution.py:29
  94.4 0.0 all-gather.4.cloned.1.call-update
  94.5 0.2 all-gather.6.cloned.1.call-start
  94.7 0.5 all-gather.6.cloned.1.call-update
  95.4 3.8 %sort.90 = (s32[384]{0:T(512)}, s32[384]{0:T(512)S(1)}) sort(s32[384]{0:T(512)S(1)} %get-tuple-element.31, s32[384]{0:T(512)S(1)} %iota.22), dimensions={0}, to_apply=%region_3.5 | sort | flops 3456 | bytes 6144 | tf_op jit(solution)/shard_map/jit(argsort)/sort | solution.py:22
  99.2 9.8 %all-gather.4.cloned.1.call-done = f32[2,768,768]{2,1,0:T(8,128)} async-done(((f32[2,384,768]{2,1,0:T(8,128)}), f32[2,768,768]{2,1,0:T(8,128)}) %all-gather.4.cloned.1.call-update) | async-done | bytes 4718608 | tf_op jit(solution)/shard_map/all_gather | solution.py:11
  109.0 7.9 %fusion.6 = f32[2,384,768]{2,1,0:T(8,128)S(1)} fusion(f32[2,768,768]{2,1,0:T(8,128)} %all-gather.4.cloned.1.call-done, f32[2,384,768]{2,1,0:T(8,128)S(1)} %copy-done.2, f32[2,768]{1,0:T(2,128)S(1)} %bitcast.48), kind=kOutput, calls=%fused_computation.19 | convolution fusion | flops 5436407808 | bytes 9443328 | tf_op jit(solution)/shard_map/hrk,hkc->hrc/dot_general | solution.py:12
  116.9 0.2 fusion.42
  117.1 0.5 maximum_select_fusion.1
  117.6 3.2 %copy.12 = f32[2,384,768]{2,0,1:T(2,128)} copy(f32[2,384,768]{2,1,0:T(8,128)S(1)} %maximum_select_fusion.1) | data formatting | bytes 4718592 | tf_op jit(solution)/shard_map/jit(_where)/select_n | solution.py:46
  120.8 5.4 %gather_fusion.2 = f32[384,2,768]{2,1,0:T(2,128)S(1)} fusion(f32[2,384,768]{2,0,1:T(2,128)} %copy.12, s32[1024]{0:T(1024)S(1)} %pad_clamp_fusion.1), kind=kCustom, calls=%fused_computation.2.clone | custom fusion | bytes 4720128 | tf_op jit(solution)/shard_map/jit(_take)/gather | solution.py:23
  126.2 2.8 %select_bitcast_fusion = f32[2,384,768]{2,0,1:T(2,128)} fusion(f32[384,2,768]{2,1,0:T(2,128)S(1)} %gather_fusion.2, pred[384]{0:T(512)(128)(4,1)S(1)} %compare_and_fusion.1), kind=kLoop, calls=%fused_computation.17 | loop fusion | flops 589824 | bytes 4718976 | tf_op jit(solution)/shard_map/jit(_take)/select_n | solution.py:23
  128.9 7.0 %all-to-all-start.1 = ((f32[2,384,768]{2,0,1:T(2,128)}), f32[2,384,768]{2,0,1:T(2,128)}, u32[]{:S(2)}, u32[]{:S(2)}) async-start(f32[2,384,768]{2,0,1:T(2,128)} %select_bitcast_fusion), calls=%async_computation.1 | async-start | bytes 4718592 | tf_op jit(solution)/shard_map/all_to_all | solution.py:51
  136.0 3.8 %sort.91 = (s32[384]{0:T(512)}, s32[384]{0:T(512)S(1)}) sort(s32[384]{0:T(512)S(1)} %get-tuple-element.30, s32[384]{0:T(512)S(1)} %iota.23), dimensions={0}, to_apply=%region_4.6 | sort | flops 3456 | bytes 6144 | tf_op jit(solution)/shard_map/jit(argsort)/sort | solution.py:27
  139.8 3.8 %sort.92 = (s32[384]{0:T(512)}, s32[384]{0:T(512)S(1)}) sort(s32[384]{0:T(512)S(1)} %get-tuple-element.16, s32[384]{0:T(512)S(1)} %iota.24), dimensions={0}, to_apply=%region_5.7 | sort | flops 3456 | bytes 6144 | tf_op jit(solution)/shard_map/jit(argsort)/sort | solution.py:28
  143.6 45.2 %all-to-all-done.1 = f32[2,384,768]{2,0,1:T(2,128)} async-done(((f32[2,384,768]{2,0,1:T(2,128)}), f32[2,384,768]{2,0,1:T(2,128)}, u32[]{:S(2)}, u32[]{:S(2)}) %all-to-all-start.1) | async-done | bytes 2359328 | tf_op jit(solution)/shard_map/all_to_all | solution.py:51
  188.8 6.3 %gather_fusion.3 = f32[384,2,768]{2,1,0:T(2,128)} fusion(f32[2,384,768]{2,0,1:T(2,128)} %all-to-all-done.1, s32[1024]{0:T(1024)S(1)} %pad_clamp_fusion), kind=kCustom, calls=%fused_computation.3.clone | custom fusion | bytes 4720128 | tf_op jit(solution)/shard_map/jit(_take)/gather | solution.py:29
  195.1 11.0 %fusion.4 = f32[2,1,1,384,768]{4,3,2,1,0:T(8,128)} fusion(f32[2,1,1,384,768]{4,3,2,1,0:T(8,128)} %param.9, f32[2,1,1,384,768]{4,3,2,1,0:T(8,128)S(1)} %copy-done.1, f32[384,2,768]{2,1,0:T(2,128)} %gather_fusion.3, f32[2,1,1,768,768]{4,3,0,2,1:T(8,128)} %all-gather.6.cloned.1.call-done, f32[2,768]{1,0:T(2,128)S(1)} %bitcast.47, ...), kind=kOutput, calls=%fused_computation.11 | convolution fusion | flops 5439356928 | bytes 14162304 | tf_op jit(solution)/shard_map/hrk,hkc->hrc/dot_general | solution.py:12
  (40 shorter events, 0.3 us)
Async XLA Ops:
  11.2 2.4 %copy-start = (f32[2,1,1,384,768]{4,3,2,1,0:T(8,128)S(1)}, f32[2,1,1,384,768]{4,3,2,1,0:T(8,128)}, u32[]{:S(2)}) copy-start(f32[2,1,1,384,768]{4,3,2,1,0:T(8,128)} %param.8) | copy-start | bytes 7077892
  25.1 60.8 %all-to-all-start = ((f32[2,384,768]{2,0,1:T(2,128)}), f32[2,384,768]{2,0,1:T(2,128)S(1)}, u32[]{:S(2)}, u32[]{:S(2)}) async-start(f32[2,384,768]{2,0,1:T(2,128)} %select_bitcast_fusion.1), calls=%async_computation | async-start | bytes 4718592 | tf_op jit(solution)/shard_map/all_to_all | solution.py:51
  33.5 75.5 %all-gather.4.cloned.1.call-start = ((), (), s32[]{:S(2)}) async-start(), calls=%async_computation.2 | async-start | bytes 7077888 | tf_op jit(solution)/shard_map/all_gather | solution.py:11
  94.4 0.8 copy-start.3
  94.4 4.7 %copy-start.4 = (f32[2,1,1,768]{3,2,1,0:T(1,128)S(1)}, f32[2,1,1,768]{3,2,1,0:T(1,128)}, u32[]{:S(2)}) copy-start(f32[2,1,1,768]{3,2,1,0:T(1,128)} %param.11) | copy-start | bytes 18436
  94.4 14.6 %copy-start.2 = (f32[2,384,768]{2,1,0:T(8,128)S(1)}, f32[2,384,768]{2,1,0:T(8,128)}, u32[]{:S(2)}) copy-start(f32[2,384,768]{2,1,0:T(8,128)} %fusion.5) | copy-start | bytes 7077892
  94.5 100.7 %all-gather.6.cloned.1.call-start = ((), (), s32[]{:S(2)}) async-start(), calls=%async_computation.3 | async-start | bytes 7077888 | tf_op jit(solution)/shard_map/all_gather | solution.py:11
  128.9 7.0 %copy-start.5 = (f32[2,1,1,768]{3,2,1,0:T(1,128)S(1)}, f32[2,1,1,768]{3,2,1,0:T(1,128)}, u32[]{:S(2)}) copy-start(f32[2,1,1,768]{3,2,1,0:T(1,128)} %param.10) | copy-start | bytes 18436
  128.9 59.9 %all-to-all-start.1 = ((f32[2,384,768]{2,0,1:T(2,128)}), f32[2,384,768]{2,0,1:T(2,128)}, u32[]{:S(2)}, u32[]{:S(2)}) async-start(f32[2,384,768]{2,0,1:T(2,128)} %select_bitcast_fusion), calls=%async_computation.1 | async-start | bytes 4718592 | tf_op jit(solution)/shard_map/all_to_all | solution.py:51
  143.6 51.5 %copy-start.1 = (f32[2,1,1,384,768]{4,3,2,1,0:T(8,128)S(1)}, f32[2,1,1,384,768]{4,3,2,1,0:T(8,128)}, u32[]{:S(2)}) copy-start(f32[2,1,1,384,768]{4,3,2,1,0:T(8,128)} %param.8) | copy-start | bytes 7077892
Sparse Core Ops, SparseCore 0:
  94.6 14.3 all-gather.3
  110.5 15.6 all-gather.5
where the time goes:
time: 213 us
  waiting for transfers between devices  100 us (47%)
  other arithmetic  32.7 us (15%)
  local copies, waits for them, and re-layouts  31.7 us (15%)
  matrix products  18.9 us (9%)
  starting transfers between devices  15.6 us (7%)
  between operations  13.6 us (6%)
    all_to_all x2, waiting for transfers between devices, crossing(): lax.all_to_all(pack_rows(turned, target_x * width_y + target_y), ('kx', '...  90 us
    dot_general x2, matrix products, ladder(): jnp.einsum('hrk,hkc->hrc', scaled, whole, precision=lax.Precision.HIGHEST...  18.9 us
    all_to_all x2, starting transfers between devices, crossing(): lax.all_to_all(pack_rows(turned, target_x * width_y + target_y), ('kx', '...  15.3 us
    gather x2, local copies, waits for them, and re-layouts, unpack_rows(): return jnp.take(data, inverse, axis=1)  11.5 us
    gather x2, local copies, waits for them, and re-layouts, pack_rows(): return jnp.take(data, row_order, axis=1)  10.4 us
    all_gather x2, waiting for transfers between devices, ladder(): whole = lax.all_gather(vertex_rows, 'af', axis=1, tiled=True)  9.83 us
    sort x2, other arithmetic, unpack_rows(): inverse = jnp.argsort(row_order, stable=True)  7.57 us
    sort x2, other arithmetic, unpack_rows(): row_order = jnp.argsort(anchor, stable=True)  7.57 us
  transfers between devices with their start and end apart: 4, of which 3 were waited for; matrix products, arithmetic and copies ran while one was open for 21% of the time, Pallas kernels for 0%

commit v1 on v0

v1 whole, which is shorter than its diff:
```python
import functools

import jax
import jax.numpy as jnp
from jax import lax
from jax.experimental import pallas as pl
from jax.experimental.pallas import tpu as pltpu
from jax.sharding import PartitionSpec as P

mixing = 0.5
LANES = 128

VMEM = pl.BlockSpec(memory_space=pltpu.VMEM)


def call(kernel, out_shape, n_in):
    return pl.pallas_call(
        kernel,
        out_shape=out_shape,
        in_specs=[VMEM] * n_in,
        out_specs=jax.tree.map(lambda _: VMEM, out_shape),
        compiler_params=pltpu.CompilerParams(vmem_limit_bytes=56 * 1024 * 1024),
    )


def split(x):
    high = x.astype(jnp.bfloat16)
    low = (x - high.astype(jnp.float32)).astype(jnp.bfloat16)
    return high, low


def dot(a, b):
    return jnp.dot(a, b, preferred_element_type=jnp.float32)


def pick(one_hot, x):
    high, low = split(x)
    return dot(one_hot, high) + dot(one_hot, low)


def to_column(rows):
    count = rows[0].shape[1]
    stacked = jnp.concatenate(rows + [jnp.zeros((LANES - len(rows), count), jnp.float32)], axis=0)
    return stacked.T


def shear_half(table_ref, half, row_count, width_x, width_y):
    first = pl.multiple_of(half * row_count, LANES)
    shift_x = table_ref[0:1, pl.ds(first, row_count)]
    shift_y = table_ref[1:2, pl.ds(first, row_count)]
    return shift_x % width_x, shift_y % width_y, shift_x // width_x


def rank_of(label_row, label_column):
    count = label_row.shape[1]
    earlier = lax.broadcasted_iota(jnp.int32, (count, count), 0) < lax.broadcasted_iota(
        jnp.int32, (count, count), 1
    )
    same = label_column == label_row
    return jnp.sum(jnp.where(earlier & same, 1.0, 0.0), axis=0, keepdims=True)


def pack_kernel(sizes, field_ref, in_ref, out_ref, packed0_ref, packed1_ref, row_ref, column_ref):
    width_x, width_y = sizes
    items, row_count, _ = field_ref.shape
    per_class = row_count // (width_x * width_y)
    kx = lax.axis_index("kx")
    ky = lax.axis_index("ky")
    af = lax.axis_index("af")
    parts = []
    for table, half in ((in_ref, af), (in_ref, 1 - af), (out_ref, af)):
        parts.append(shear_half(table, half, row_count, width_x, width_y))
    labels = [(dx * width_y + dy).astype(jnp.float32) for dx, dy, _ in parts]
    label_columns = to_column(labels)
    rows = []
    for n, (dx, dy, turn) in enumerate(parts):
        rank = rank_of(labels[n], label_columns[:, n : n + 1]).astype(jnp.int32)
        target = ((kx + dx) % width_x) * width_y + (ky + dy) % width_y
        anchor = ((kx - dx) % width_x) * width_y + (ky - dy) % width_y
        leave = (turn + (kx + dx >= width_x).astype(jnp.int32)) % items
        arrive = (turn + (kx < dx).astype(jnp.int32)) % items
        rows.append([v.astype(jnp.float32) for v in (target * per_class + rank, anchor * per_class + rank, leave, arrive)])
    own_in, other_in, own_out = rows
    columns = to_column([own_in[1], other_in[1], own_out[1], own_out[3], own_in[2]])
    column_ref[...] = columns
    row_ref[...] = jnp.concatenate([own_in[0], own_out[0]] + [jnp.zeros((6, row_count), jnp.float32)], axis=0)
    iota = lax.broadcasted_iota(jnp.int32, (row_count, row_count), 0).astype(jnp.float32)
    one_hot = (iota == own_in[0]).astype(jnp.bfloat16)
    stay = columns[:, 4:5] == 0.0
    first, second = field_ref[0], field_ref[1]
    packed0_ref[...] = pick(one_hot, jnp.where(stay, first, second))
    packed1_ref[...] = pick(one_hot, jnp.where(stay, second, first))


def product(left, own, other):
    width = left.shape[1] // 2
    lower = lax.axis_index("af") == 0
    first = jnp.where(lower, left[:, :width], left[:, width:])
    second = jnp.where(lower, left[:, width:], left[:, :width])
    left_high, left_low = split(jnp.concatenate([first, second], axis=1))
    right_high = jnp.concatenate([own[0], other[0]], axis=0)
    right_low = jnp.concatenate([own[1], other[1]], axis=0)
    return dot(left_high, right_high) + dot(left_low, right_high) + dot(left_high, right_low)


def direct_kernel(field_ref, other_ref, bare_ref, bubble_ref, total_ref):
    for item in range(field_ref.shape[0]):
        field = field_ref[item]
        direct = product(field * bubble_ref[item : item + 1, :], split(field), split(other_ref[item]))
        total_ref[item] = (1.0 - mixing) * field + mixing * (bare_ref[item] + direct)


def unpacked(one_hot, x):
    high, low = split(x)
    return dot(one_hot, high).astype(jnp.bfloat16), dot(one_hot, low).astype(jnp.bfloat16)


def crossed_kernel(item, own_ref, other_ref, bubble_ref, row_ref, column_ref, packed_ref):
    row_count = own_ref.shape[0]
    lane = lax.broadcasted_iota(jnp.int32, (row_count, row_count), 1).astype(jnp.float32)
    sublane = lax.broadcasted_iota(jnp.int32, (row_count, row_count), 0).astype(jnp.float32)
    own = unpacked((lane == column_ref[:, 0:1]).astype(jnp.bfloat16), own_ref[...])
    other = unpacked((lane == column_ref[:, 1:2]).astype(jnp.bfloat16), other_ref[...])
    pack = (sublane == row_ref[1:2, :]).astype(jnp.bfloat16)
    left = dot(pack, own[0]) + dot(pack, own[1])
    packed_ref[...] = product(left * bubble_ref[item : item + 1, :], own, other)


def final_kernel(first_ref, second_ref, total_ref, column_ref, updated_ref):
    row_count = first_ref.shape[0]
    lane = lax.broadcasted_iota(jnp.int32, (row_count, row_count), 1).astype(jnp.float32)
    unpack = (lane == column_ref[:, 2:3]).astype(jnp.bfloat16)
    stay = column_ref[:, 3:4] == 0.0
    first = pick(unpack, first_ref[...])
    second = pick(unpack, second_ref[...])
    updated_ref[0] = total_ref[0] + mixing * jnp.where(stay, first, second)
    updated_ref[1] = total_ref[1] + mixing * jnp.where(stay, second, first)


def exchange(data):
    return lax.all_to_all(data, ("kx", "ky"), split_axis=0, concat_axis=0, tiled=True)


def swap(data):
    return lax.ppermute(data, "af", [(0, 1), (1, 0)])


def body(vertex, bare_vertex, bubble_direct, bubble_crossed, shear_in, shear_out):
    items, row_count, columns = vertex.shape[0], vertex.shape[3], vertex.shape[4]
    field = vertex.reshape(items, row_count, columns)
    bare = bare_vertex.reshape(items, row_count, columns)
    direct_bubble = bubble_direct.reshape(items, columns)
    crossed_bubble = bubble_crossed.reshape(items, columns)
    sizes = (lax.axis_size("kx"), lax.axis_size("ky"))
    whole = jax.ShapeDtypeStruct((items, row_count, columns), jnp.float32)
    block = jax.ShapeDtypeStruct((row_count, columns), jnp.float32)
    packed0, packed1, row_table, column_table = call(
        functools.partial(pack_kernel, sizes),
        (
            block,
            block,
            jax.ShapeDtypeStruct((8, row_count), jnp.float32),
            jax.ShapeDtypeStruct((row_count, LANES), jnp.float32),
        ),
        3,
    )(field, shear_in, shear_out)
    arrived0 = exchange(packed0)
    arrived1 = exchange(packed1)
    other_field = swap(field)
    total = call(direct_kernel, whole, 4)(field, other_field, bare, direct_bubble)
    back = []
    for item, arrived in enumerate((arrived0, arrived1)):
        other = swap(arrived)
        packed = call(functools.partial(crossed_kernel, item), block, 5)(
            arrived, other, crossed_bubble, row_table, column_table
        )
        back.append(exchange(packed))
    updated = call(final_kernel, whole, 4)(back[0], back[1], total, column_table)
    return updated.reshape(vertex.shape)


def solution(mesh):
    placed = (
        P(None, "kx", "ky", "af", None),
        P(None, "kx", "ky", "af", None),
        P(None, "kx", "ky", None),
        P(None, "kx", "ky", None),
        P(),
        P(),
    )
    return jax.shard_map(
        body, mesh=mesh, in_specs=placed, out_specs=P(None, "kx", "ky", "af", None), check_vma=False
    )
```

time: 213 us -> 146 us (0.69)
  waiting for transfers between devices: 100 us -> 56.8 us
  blocking collectives: 0 us -> 38.3 us
  other arithmetic: 32.7 us -> 0 us
  Pallas kernels: 0 us -> 31.9 us
  local copies, waits for them, and re-layouts: 31.7 us -> 5.32 us
  matrix products: 18.9 us -> 0 us
  between operations: 13.6 us -> 0.09 us
  starting transfers between devices: 15.6 us -> 12.9 us
    all_to_all x0 -> x1, blocking collectives: none -> 38.3 us  [exchange(): lax.all_to_all(data, ('kx', 'ky'), split_axis=0, concat_axis=0, tiled=True)]
    all_to_all x2 -> x3, waiting for transfers between devices: 90 us -> 52.1 us  [exchange(): lax.all_to_all(data, ('kx', 'ky'), split_axis=0, concat_axis=0, tiled=True)]
    pallas_call x0 -> x5, Pallas kernels: none -> 31.9 us  [the longest x2 14.1 us: body(): call(functools.partial(crossed_kernel, item), block, 5)]
    sort x6 -> x0, other arithmetic: 22.7 us -> none  [the longest x2 7.57 us: unpack_rows(): inverse = jnp.argsort(row_order, stable=True)]
    gather x4 -> x0, local copies, waits for them, and re-layouts: 21.9 us -> none  [the longest x2 11.5 us: unpack_rows(): return jnp.take(data, inverse, axis=1)]
    dot_general x2 -> x0, matrix products: 18.9 us -> none  [ladder(): jnp.einsum('hrk,hkc->hrc', scaled, whole, precision=lax.Precision.HIGHEST...]
    select_n x9 -> x0, other arithmetic: 9.85 us -> none  [the longest x4 5.53 us: pack_rows(): return jnp.take(data, row_order, axis=1)]
    all_gather x2 -> x0, waiting for transfers between devices: 9.83 us -> none  [ladder(): whole = lax.all_gather(vertex_rows, 'af', axis=1, tiled=True)]
  transfers between devices with their start and end apart: 4 -> 6, of which waited for: 3 -> 5; matrix products, arithmetic and copies ran while one was open for 21% -> 1% of each run, Pallas kernels for 0% -> 15%
where the time goes in v1:
time: 146 us; the launch traced here: 145 us
  waiting for transfers between devices  56.8 us (39%)
  blocking collectives  38.3 us (26%)
  Pallas kernels  31.9 us (22%)
  starting transfers between devices  12.9 us (9%)
  local copies, waits for them, and re-layouts  5.32 us (4%)
    all_to_all x3, waiting for transfers between devices, exchange(): lax.all_to_all(data, ('kx', 'ky'), split_axis=0, concat_axis=0, tiled=True)  52.1 us
    all_to_all x1, blocking collectives, exchange(): lax.all_to_all(data, ('kx', 'ky'), split_axis=0, concat_axis=0, tiled=True)  38.3 us
    pallas_call x2, Pallas kernels, body(): call(functools.partial(crossed_kernel, item), block, 5)  14.1 us
    all_to_all x3, starting transfers between devices, exchange(): lax.all_to_all(data, ('kx', 'ky'), split_axis=0, concat_axis=0, tiled=True)  12.2 us
    pallas_call x1, Pallas kernels, body(): call(direct_kernel, whole, 4)(field, other_field, bare, direct_bubble)  7.68 us
    pallas_call x1, Pallas kernels, body(): call(final_kernel, whole, 4)(back[0], back[1], total, column_table)  5.32 us
    unnamed x18, local copies, waits for them, and re-layouts  5.32 us
    pallas_call x1, Pallas kernels, body(): call(functools.partial(pack_kernel, sizes), (block, block, jax.ShapeDtype...  4.82 us
  transfers between devices with their start and end apart: 6, of which 5 were waited for; matrix products, arithmetic and copies ran while one was open for 1% of the time, Pallas kernels for 15%

profile of v1, /device:TPU:0, one launch (start us, length us, event | category | flops | bytes accessed | tf_op | source)
XLA Modules:
  0.0 145.3 jit_solution(6042700871613095040)
XLA Ops:
  0.0 4.8 %shard_map.64 = (f32[384,768]{1,0:T(8,128)}, f32[384,768]{1,0:T(8,128)}, f32[8,384]{1,0:T(8,128)}, f32[384,128]{1,0:T(8,128)}) custom-call(f32[2,384,768]{2,1,0:T(8,128)} %bitcast.19, s32[2,768]{1,0:T(2,128)} %in_ref.1, s32[2,768]{1,0:T(2,128)} %out_ref.1), custom_call_target="tpu_custom_call" | custom-call | tf_op jit(solution)/shard_map/pallas_call | solution.py:157
  4.8 38.3 %all_to_all.44 = f32[16,24,768]{2,1,0:T(8,128)S(1)} all-to-all(f32[16,24,768]{2,1,0:T(8,128)} %bitcast.30), channel_id=1, replica_groups=mesh['kx'=2,'ky'=8,'af'=2] {'kx','ky'}, dimensions={0} | all-to-all | bytes 2359296 | tf_op jit(solution)/shard_map/all_to_all | solution.py:141
  43.1 0.0 copy-start.3
  43.1 0.0 copy-start.6
  43.1 3.8 %all-to-all-start = ((f32[16,24,768]{2,1,0:T(8,128)}), f32[16,24,768]{2,1,0:T(8,128)S(1)}, u32[]{:S(2)}, u32[]{:S(2)}) async-start(f32[16,24,768]{2,1,0:T(8,128)} %bitcast.1), calls=%async_computation | async-start | bytes 2359296 | tf_op jit(solution)/shard_map/all_to_all | solution.py:141
  47.0 0.0 copy-done.3
  47.0 0.1 collective-permute-start.1
  47.1 0.0 copy-done.6
  47.1 0.6 copy.13
  47.7 2.2 %collective-permute-done.1.other_ref = f32[384,768]{1,0:T(8,128)S(1)} collective-permute-done((f32[384,768]{1,0:T(8,128)S(1)}, f32[384,768]{1,0:T(8,128)S(1)}, u32[]{:S(2)}, u32[]{:S(2)}) %collective-permute-start.1) | collective-permute-done | bytes 1179680 | tf_op jit(solution)/shard_map/ppermute | solution.py:145
  49.9 0.0 copy-start.5
  49.9 1.0 copy-done.5
  50.9 7.1 %shard_map.66 = f32[384,768]{1,0:T(8,128)} custom-call(f32[384,768]{1,0:T(8,128)} %bitcast.28, f32[384,768]{1,0:T(8,128)} %copy-done.5, f32[2,768]{1,0:T(2,128)} %bitcast.31, f32[8,384]{1,0:T(8,128)} %get-tuple-element.10.row_ref, f32[384,128]{1,0:T(8,128)} %get-tuple-element.11.column_ref), custom_call_target="tpu_custom_call" | custom-call | tf_op jit(solution)/shard_map/pallas_call | solution.py:174
  58.0 16.8 %all-to-all-done = f32[16,24,768]{2,1,0:T(8,128)S(1)} async-done(((f32[16,24,768]{2,1,0:T(8,128)}), f32[16,24,768]{2,1,0:T(8,128)S(1)}, u32[]{:S(2)}, u32[]{:S(2)}) %all-to-all-start) | async-done | bytes 1179680 | tf_op jit(solution)/shard_map/all_to_all | solution.py:141
  74.7 0.0 copy-start.2
  74.7 1.0 copy-done.2
  75.7 3.8 %all-to-all-start.3 = ((f32[16,24,768]{2,1,0:T(8,128)}), f32[16,24,768]{2,1,0:T(8,128)S(1)}, u32[]{:S(2)}, u32[]{:S(2)}) async-start(f32[16,24,768]{2,1,0:T(8,128)} %bitcast.25), calls=%async_computation.3 | async-start | bytes 2359296 | tf_op jit(solution)/shard_map/all_to_all | solution.py:141
  79.6 0.1 collective-permute-start
  79.7 0.0 copy-done
  79.7 0.5 collective-permute-start.2
  80.2 2.5 %collective-permute-done.other_ref = f32[384,768]{1,0:T(8,128)S(1)} collective-permute-done((f32[384,768]{1,0:T(8,128)}, f32[384,768]{1,0:T(8,128)S(1)}, u32[]{:S(2)}, u32[]{:S(2)}) %collective-permute-start) | collective-permute-done | bytes 1179680 | tf_op jit(solution)/shard_map/ppermute | solution.py:145
  82.7 1.0 copy-done.4
  83.7 7.0 %shard_map.65 = f32[384,768]{1,0:T(8,128)} custom-call(f32[384,768]{1,0:T(8,128)} %bitcast.24, f32[384,768]{1,0:T(8,128)} %copy-done.4, f32[2,768]{1,0:T(2,128)} %bitcast.32, f32[8,384]{1,0:T(8,128)} %get-tuple-element.10.row_ref, f32[384,128]{1,0:T(8,128)} %get-tuple-element.11.column_ref), custom_call_target="tpu_custom_call" | custom-call | tf_op jit(solution)/shard_map/pallas_call | solution.py:174
  90.8 16.6 %all-to-all-done.3 = f32[16,24,768]{2,1,0:T(8,128)S(1)} async-done(((f32[16,24,768]{2,1,0:T(8,128)}), f32[16,24,768]{2,1,0:T(8,128)S(1)}, u32[]{:S(2)}, u32[]{:S(2)}) %all-to-all-start.3) | async-done | bytes 1179680 | tf_op jit(solution)/shard_map/all_to_all | solution.py:141
  107.3 1.1 copy-done.1
  108.4 4.6 %all-to-all-start.1 = ((f32[16,24,768]{2,1,0:T(8,128)}), f32[16,24,768]{2,1,0:T(8,128)}, u32[]{:S(2)}, u32[]{:S(2)}) async-start(f32[16,24,768]{2,1,0:T(8,128)} %bitcast.26), calls=%async_computation.1 | async-start | bytes 2359296 | tf_op jit(solution)/shard_map/all_to_all | solution.py:141
  113.0 0.0 copy-done.7
  113.0 0.6 copy.12
  113.6 0.0 collective-permute-done.2.other_ref
  113.6 7.7 %shard_map.67.total_ref = f32[2,384,768]{2,1,0:T(8,128)} custom-call(f32[2,384,768]{2,1,0:T(8,128)} %bitcast.20, f32[2,384,768]{2,1,0:T(8,128)} %collective-permute-done.2.other_ref, f32[2,384,768]{2,1,0:T(8,128)} %bitcast.29, f32[2,768]{1,0:T(2,128)} %bitcast.33), custom_call_target="tpu_custom_call" | custom-call | tf_op jit(solution)/shard_map/pallas_call | solution.py:170
  121.3 18.7 %all-to-all-done.1 = f32[16,24,768]{2,1,0:T(8,128)} async-done(((f32[16,24,768]{2,1,0:T(8,128)}), f32[16,24,768]{2,1,0:T(8,128)}, u32[]{:S(2)}, u32[]{:S(2)}) %all-to-all-start.1) | async-done | bytes 1179680 | tf_op jit(solution)/shard_map/all_to_all | solution.py:141
  140.0 5.3 %shard_map.68 = f32[2,384,768]{2,1,0:T(8,128)} custom-call(f32[384,768]{1,0:T(8,128)} %bitcast.4.first_ref, f32[384,768]{1,0:T(8,128)} %bitcast.22, f32[2,384,768]{2,1,0:T(8,128)} %shard_map.67.total_ref, f32[384,128]{1,0:T(8,128)} %get-tuple-element.11.column_ref), custom_call_target="tpu_custom_call" | custom-call | tf_op jit(solution)/shard_map/pallas_call | solution.py:178
  (4 shorter events, 0.0 us)
Async XLA Ops:
  43.1 3.8 %copy-start.3 = (f32[16,24,768]{2,1,0:T(8,128)}, f32[16,24,768]{2,1,0:T(8,128)S(1)}, u32[]{:S(2)}) copy-start(f32[16,24,768]{2,1,0:T(8,128)S(1)} %all_to_all.44) | copy-start | bytes 3538948
  43.1 3.9 %copy-start.6 = (f32[2,1,1,768]{3,2,1,0:T(1,128)S(1)}, f32[2,1,1,768]{3,2,1,0:T(1,128)}, u32[]{:S(2)}) copy-start(f32[2,1,1,768]{3,2,1,0:T(1,128)} %param.9) | copy-start | bytes 18436
  43.1 31.6 %all-to-all-start = ((f32[16,24,768]{2,1,0:T(8,128)}), f32[16,24,768]{2,1,0:T(8,128)S(1)}, u32[]{:S(2)}, u32[]{:S(2)}) async-start(f32[16,24,768]{2,1,0:T(8,128)} %bitcast.1), calls=%async_computation | async-start | bytes 2359296 | tf_op jit(solution)/shard_map/all_to_all | solution.py:141
  47.0 2.9 %collective-permute-start.1 = (f32[384,768]{1,0:T(8,128)S(1)}, f32[384,768]{1,0:T(8,128)S(1)}, u32[]{:S(2)}, u32[]{:S(2)}) collective-permute-start(f32[384,768]{1,0:T(8,128)S(1)} %bitcast.27), channel_id=1, source_target_pairs={{0,1},{1,0},{2,3},{3,2},{4,5},{5,4},{6,7},{7,6},{8,9},{9,8},{10,11... | collective-permute-start | bytes 3538952 | tf_op jit(solution)/shard_map/ppermute | solution.py:145
  49.9 1.0 copy-start.5
  74.7 1.0 copy-start.2
  75.7 3.9 %copy-start = (f32[2,1,1,384,768]{4,3,2,1,0:T(8,128)S(1)}, f32[2,1,1,384,768]{4,3,2,1,0:T(8,128)}, u32[]{:S(2)}) copy-start(f32[2,1,1,384,768]{4,3,2,1,0:T(8,128)} %param.6) | copy-start | bytes 7077892
  75.7 31.6 %all-to-all-start.3 = ((f32[16,24,768]{2,1,0:T(8,128)}), f32[16,24,768]{2,1,0:T(8,128)S(1)}, u32[]{:S(2)}, u32[]{:S(2)}) async-start(f32[16,24,768]{2,1,0:T(8,128)} %bitcast.25), calls=%async_computation.3 | async-start | bytes 2359296 | tf_op jit(solution)/shard_map/all_to_all | solution.py:141
  79.6 3.1 %collective-permute-start = (f32[384,768]{1,0:T(8,128)}, f32[384,768]{1,0:T(8,128)S(1)}, u32[]{:S(2)}, u32[]{:S(2)}) collective-permute-start(f32[384,768]{1,0:T(8,128)} %bitcast.23), channel_id=1, source_target_pairs={{0,1},{1,0},{2,3},{3,2},{4,5},{5,4},{6,7},{7,6},{8,9},{9,8},{10,11... | collective-permute-start | bytes 3538952 | tf_op jit(solution)/shard_map/ppermute | solution.py:145
  79.7 33.9 %collective-permute-start.2 = (f32[2,384,768]{2,1,0:T(8,128)S(1)}, f32[2,384,768]{2,1,0:T(8,128)}, u32[]{:S(2)}, u32[]{:S(2)}) collective-permute-start(f32[2,384,768]{2,1,0:T(8,128)S(1)} %bitcast.21), channel_id=1, source_target_pairs={{0,1},{1,0},{2,3},{3,2},{4,5},{5,4},{6,7},{7,6},{8,9},{9,8},{10,11... | collective-permute-start | bytes 7077896 | tf_op jit(solution)/shard_map/ppermute | solution.py:145
  82.7 1.0 copy-start.4
  107.3 1.1 copy-start.1
  107.3 5.6 %copy-start.7 = (f32[2,1,1,768]{3,2,1,0:T(1,128)S(1)}, f32[2,1,1,768]{3,2,1,0:T(1,128)}, u32[]{:S(2)}) copy-start(f32[2,1,1,768]{3,2,1,0:T(1,128)} %param.8) | copy-start | bytes 18436
  108.4 31.6 %all-to-all-start.1 = ((f32[16,24,768]{2,1,0:T(8,128)}), f32[16,24,768]{2,1,0:T(8,128)}, u32[]{:S(2)}, u32[]{:S(2)}) async-start(f32[16,24,768]{2,1,0:T(8,128)} %bitcast.26), calls=%async_computation.1 | async-start | bytes 2359296 | tf_op jit(solution)/shard_map/all_to_all | solution.py:141
